TPU v7x, 32 devices: a whole 2x2x4 slice. The times are simulated.
32 devices in a mesh: seq: 8 (over z, y), head: 4 (over x, core).
Axes of the slice: x: 2, y: 2, z: 4, core: 2. Of those that a mesh axis runs over, the one named last changes fastest.
Arguments:
- queries: bfloat16 [4096, 4096], P('seq', 'head'), may hold values from -6 to 6
- keys: bfloat16 [4096, 4096], P('seq', 'head'), may hold values from -6 to 6
- values: bfloat16 [4096, 4096], P('seq', 'head'), may hold values from -6 to 6
- level_weights: float32 [5, 32, 4096], P(None, 'head', 'seq'), may hold values from 0.1 to 3, as said below
- norm_gain: float32 [4096], P('head'), may hold values from 0.25 to 1.75
Outputs:
- mixed: bfloat16 [4096, 4096], P('seq', 'head')
Inputs may be any that keep to these rules, and one draw needn't show every extreme that they name: `level_weights`: positive level weights.
All inputs are finite; a program needn't handle non-finite values.
Results may differ from a plain program's by a relative error of at most 0.0049.
Values may be sent and summed in bfloat16 or wider, within the bound.
No kernel may reach another device: no remote copies, remote signals or barrier semaphores. Data moves between devices by JAX's collectives and lax.ppermute only.
A program may use at most 64 MiB of HBM per device.

v0:
```python
import jax
import jax.numpy as jnp
from jax import lax
from jax.sharding import PartitionSpec as P

HEAD_DIM = 128
STRETCH = 256
D = 4096
EPSILON = 1e-06


def swapped(block, axis, stride):
    count = lax.axis_size(axis)
    route = []
    for low in range(count):
        high = low | 1 << stride
        if high != low and high < count:
            route += [(low, high), (high, low)]
    return lax.ppermute(block, axis, route)


def shifted(block, axis, distance):
    devices = range(lax.axis_size(axis))
    route = [(i - distance, i) for i in devices if i - distance in devices]
    return lax.ppermute(block, axis, route)


def local(queries, keys, values, level_weights, norm_gain):
    tok_rows = queries.shape[0]
    heads_here = queries.shape[1] // HEAD_DIM
    stretch_count = tok_rows // STRETCH
    block_shape = (stretch_count, STRETCH, heads_here, HEAD_DIM)
    query_block_list = queries.reshape(block_shape)
    key_blocks = keys.reshape(block_shape)
    value_blocks = values.reshape(block_shape)
    level_total = level_weights.shape[0]
    weights_here = level_weights.reshape(level_total, heads_here, stretch_count, STRETCH).transpose(
        0, 2, 3, 1
    )
    states = jnp.einsum(
        "cthk,cthv->chkv", key_blocks, value_blocks, preferred_element_type=jnp.float32
    )
    scores = jnp.einsum(
        "cthk,cshk->chts", query_block_list, key_blocks, preferred_element_type=jnp.float32
    )
    causal = lax.broadcasted_iota(jnp.int32, (STRETCH, STRETCH), 0) >= lax.broadcasted_iota(
        jnp.int32, (STRETCH, STRETCH), 1
    )
    attn_probs = jnp.where(causal[None, None], scores, 0.0).astype(jnp.bfloat16)
    intra_out = jnp.einsum(
        "chts,cshv->cthv", attn_probs, value_blocks, preferred_element_type=jnp.float32
    )
    combined = weights_here[0][..., None] * intra_out
    running = states
    local_bits = stretch_count.bit_length() - 1
    level_bit = 0
    groups = running.shape[0] // 2
    block_span = 2**level_bit
    halves = running.reshape(groups, 2, heads_here, HEAD_DIM, HEAD_DIM)
    leftward_sum = halves[:, 0].astype(jnp.bfloat16)
    rightward_queries = query_block_list.reshape(
        groups, 2, block_span * STRETCH, heads_here, HEAD_DIM
    )[:, 1]
    state_readout = jnp.einsum(
        "nthk,nhkv->nthv", rightward_queries, leftward_sum, preferred_element_type=jnp.float32
    )
    level_weight = weights_here[1 + level_bit].reshape(groups, 2, block_span * STRETCH, heads_here)[
        :, 1
    ]
    contrib = level_weight[..., None] * state_readout
    padded = jnp.stack([jnp.zeros_like(contrib), contrib], axis=1)
    combined = combined + padded.reshape(stretch_count, STRETCH, heads_here, HEAD_DIM)
    running = halves[:, 0] + halves[:, 1]
    device_sum = running[0]
    seq_count = lax.axis_size("seq")
    seq_bits = seq_count.bit_length() - 1
    position = lax.axis_index("seq")
    crossing_state_list = []
    for level_bit in range(seq_bits - 1):
        partner = swapped(device_sum, "seq", level_bit)
        is_right = position >> level_bit & 1 == 1
        crossing_state_list.append(
            jnp.where(is_right, partner, jnp.zeros_like(partner)).astype(jnp.bfloat16)
        )
        device_sum = device_sum + partner
    last_partner = shifted(device_sum.astype(jnp.bfloat16), "seq", seq_count // 2)
    crossing_state_list.append(last_partner)
    for number, state_per_level in enumerate(crossing_state_list):
        state_readout = jnp.einsum(
            "lwnx,nxq->lwnq", query_block_list, state_per_level, preferred_element_type=jnp.float32
        )
        combined = combined + weights_here[1 + local_bits + number][..., None] * state_readout
    squares = jnp.sum(combined * combined, axis=(2, 3)).reshape(tok_rows)
    total_squares = lax.psum(squares, "head")
    inverse_rms = lax.rsqrt(total_squares / D + EPSILON)
    flat_out = combined.reshape(tok_rows, heads_here * HEAD_DIM)
    mixed_out = flat_out * inverse_rms[:, None] * norm_gain[None, :]
    return mixed_out.astype(jnp.bfloat16)


def solution(mesh):
    return jax.shard_map(
        local,
        mesh=mesh,
        in_specs=(
            P("seq", "head"),
            P("seq", "head"),
            P("seq", "head"),
            P(None, "head", "seq"),
            P("head"),
        ),
        out_specs=P("seq", "head"),
        check_vma=False,
    )
```

profile of v0, /device:TPU:24, one launch (start us, length us, event | category | flops | bytes accessed | tf_op | source)
XLA Modules:
  0.0 59.7 jit_solution(3533077832521115567)
XLA Ops:
  0.0 1.6 %copy.53 = bf16[64,8,8,128]{3,2,1,0:T(8,128)(2,1)S(1)} copy(bf16[64,8,8,128]{3,1,2,0:T(8,128)(2,1)} %bitcast.103) | data formatting | bytes 2097152
  1.6 0.7 %copy.20 = bf16[2,256,8,128]{1,3,2,0:T(8,128)(2,1)S(1)} copy(bf16[2,256,8,128]{3,2,1,0:T(8,128)(2,1)S(1)} %bitcast.102) | data formatting | bytes 2097152 | tf_op jit(solution)/shard_map/reshape | solution.py:34
  2.3 0.0 copy-start
  2.3 0.3 copy.54
  2.6 0.4 convolution_bitcast_fusion.1
  3.0 0.2 copy-done
  3.2 0.8 %fusion.17 = f32[8,128,128]{2,1,0:T(8,128)} fusion(f32[1,2,8,128,128]{4,3,2,1,0:T(8,128)S(1)} %convolution_bitcast_fusion.1), kind=kLoop, calls=%fused_computation.27 | loop fusion | flops 131072 | bytes 1572864 | tf_op jit(solution)/shard_map/add | solution.py:73
  4.1 1.5 %collective-permute-start = (f32[8,128,128]{2,1,0:T(8,128)}, f32[8,128,128]{2,1,0:T(8,128)}, u32[]{:S(2)}, u32[]{:S(2)}) collective-permute-start(f32[8,128,128]{2,1,0:T(8,128)} %fusion.17), channel_id=1, source_target_pairs={{0,4},{4,0},{8,12},{12,8},{16,20},{20,16},{24,28},{28,24},{1,5},{5... | collective-permute-start | bytes 1572872 | tf_op jit(solution)/shard_map/ppermute | solution.py:19
  5.7 0.3 copy.52
  6.0 0.3 fusion.7
  6.4 4.2 %fusion.5 = f32[2,8,256,128]{2,3,1,0:T(8,128)} fusion(bf16[2,256,8,128]{1,3,2,0:T(8,128)(2,1)} %copy-done, pred[256,256]{1,0:T(8,128)(4,1)S(1)} %iota_compare_fusion, bf16[2,256,8,128]{3,2,1,0:T(8,128)(2,1)} %bitcast.101, bf16[2,256,8,128]{3,2,1,0:T(8,128)(2,1)S(1)} %bitcast.95), kind=kOutput, calls=%fused_computation.13 | convolution fusion | flops 538968064 | bytes 5308416 | tf_op jit(solution)/shard_map/chts,cshv->cthv/dot_general | solution.py:50
  10.6 7.5 %collective-permute-done = f32[8,128,128]{2,1,0:T(8,128)} collective-permute-done((f32[8,128,128]{2,1,0:T(8,128)}, f32[8,128,128]{2,1,0:T(8,128)}, u32[]{:S(2)}, u32[]{:S(2)}) %collective-permute-start) | collective-permute-done | bytes 524320 | tf_op jit(solution)/shard_map/ppermute | solution.py:19
  18.1 1.1 %fusion.34 = f32[8,128,128]{2,1,0:T(8,128)S(1)} fusion(f32[8,128,128]{2,1,0:T(8,128)} %collective-permute-done, f32[1,2,8,128,128]{4,3,2,1,0:T(8,128)S(1)} %convolution_bitcast_fusion.1), kind=kLoop, calls=%fused_computation.51 | loop fusion | flops 262144 | bytes 2097152 | tf_op jit(solution)/shard_map/add | solution.py:85
  19.2 0.5 collective-permute-start.1
  19.7 0.5 fusion.13
  20.2 11.8 %collective-permute-done.1 = f32[8,128,128]{2,1,0:T(8,128)S(1)} collective-permute-done((f32[8,128,128]{2,1,0:T(8,128)S(1)}, f32[8,128,128]{2,1,0:T(8,128)S(1)}, u32[]{:S(2)}, u32[]{:S(2)}) %collective-permute-start.1) | collective-permute-done | bytes 524320 | tf_op jit(solution)/shard_map/ppermute | solution.py:19
  32.1 0.1 add_convert_fusion
  32.1 1.4 %collective-permute-start.2 = (bf16[8,128,128]{2,1,0:T(8,128)(2,1)S(1)}, bf16[8,128,128]{2,1,0:T(8,128)(2,1)S(1)}, u32[]{:S(2)}, u32[]{:S(2)}) collective-permute-start(bf16[8,128,128]{2,1,0:T(8,128)(2,1)S(1)} %add_convert_fusion), channel_id=1, source_target_pairs={{0,16},{4,20},{8,24},{12,28},{1,17},{5,21},{9,25},{13,29},{2,18},{... | collective-permute-start | bytes 786440 | tf_op jit(solution)/shard_map/ppermute | solution.py:25
  33.6 0.5 fusion.11
  34.1 12.8 %collective-permute-done.2 = bf16[8,128,128]{2,1,0:T(8,128)(2,1)S(1)} collective-permute-done((bf16[8,128,128]{2,1,0:T(8,128)(2,1)S(1)}, bf16[8,128,128]{2,1,0:T(8,128)(2,1)S(1)}, u32[]{:S(2)}, u32[]{:S(2)}) %collective-permute-start.2) | collective-permute-done | bytes 262176 | tf_op jit(solution)/shard_map/ppermute | solution.py:25
  46.9 2.4 %multiply_reduce_fusion = (f32[2,256]{1,0:T(2,128)S(1)}, f32[2,256,8,128]{1,3,2,0:T(8,128)}) fusion(bf16[2,256,8,128]{3,2,1,0:T(8,128)(2,1)S(1)} %bitcast.98, bf16[8,128,128]{2,1,0:T(8,128)(2,1)S(1)} %collective-permute-done.2, f32[2,256,8]{1,2,0:T(8,128)S(1)} %get-tuple-element.6, f32[8,128,2,256]{3,1,0,2:T(8,128)S(1)} %fusion.11, ...), kind=kOutput, calls=%fused_computation.12 | convolution fusion | flops 139460096 | bytes 10815488 | tf_op jit(solution)/shard_map/lwnx,nxq->lwnq/dot_general | solution.py:89
  49.3 6.8 %psum.7 = f32[512]{0:T(512)S(1)} all-reduce(f32[512]{0:T(512)S(1)} %bitcast.109), channel_id=1, replica_groups=mesh['seq'=8,'head'=4] {'head'}, use_global_device_ids=true, to_apply=%region_1.2 | all-reduce | flops 512 | bytes 4096 | tf_op jit(solution)/shard_map/psum | solution.py:94
  56.1 2.1 %copy.33 = f32[2,256,8,128]{3,2,1,0:T(8,128)S(1)} copy(f32[2,256,8,128]{1,3,2,0:T(8,128)} %get-tuple-element.10) | data formatting | bytes 4194304 | tf_op jit(solution)/shard_map/add | solution.py:92
  58.3 1.4 %fusion.1 = bf16[512,1024]{1,0:T(8,128)(2,1)} fusion(f32[64,8,8,128]{3,2,1,0:T(8,128)S(1)} %bitcast.99, f32[1024]{0:T(1024)S(1)} %copy-done.6, f32[512]{0:T(512)S(1)} %add_rsqrt_fusion), kind=kLoop, calls=%fused_computation.3 | loop fusion | flops 1572864 | bytes 3151872 | tf_op jit(solution)/shard_map/convert_element_type | solution.py:98
  (18 shorter events, 0.1 us)
Async XLA Ops:
  0.0 2.3 %copy-start.3 = (bf16[512,1024]{1,0:T(8,128)(2,1)S(1)}, bf16[512,1024]{1,0:T(8,128)(2,1)}, u32[]{:S(2)}) copy-start(bf16[512,1024]{1,0:T(8,128)(2,1)} %param.7) | copy-start | bytes 3145732
  2.3 1.0 %copy-start = (bf16[2,256,8,128]{1,3,2,0:T(8,128)(2,1)}, bf16[2,256,8,128]{1,3,2,0:T(8,128)(2,1)S(1)}, u32[]{:S(2)}) copy-start(bf16[2,256,8,128]{1,3,2,0:T(8,128)(2,1)S(1)} %copy.20) | copy-start | bytes 3145732
  2.6 1.5 %copy-start.1 = (bf16[64,8,8,128]{3,2,1,0:T(8,128)(2,1)}, bf16[64,8,8,128]{3,2,1,0:T(8,128)(2,1)S(1)}, u32[]{:S(2)}) copy-start(bf16[64,8,8,128]{3,2,1,0:T(8,128)(2,1)S(1)} %copy.54) | copy-start | bytes 3145732
  2.6 3.1 %copy-start.5 = (f32[5,8,512]{2,1,0:T(8,128)S(1)}, f32[5,8,512]{2,1,0:T(8,128)}, u32[]{:S(2)}) copy-start(f32[5,8,512]{2,1,0:T(8,128)} %param.8) | copy-start | bytes 245764
  2.6 3.1 %copy-start.4 = (bf16[512,1024]{1,0:T(8,128)(2,1)S(1)}, bf16[512,1024]{1,0:T(8,128)(2,1)}, u32[]{:S(2)}) copy-start(bf16[512,1024]{1,0:T(8,128)(2,1)} %param.5) | copy-start | bytes 3145732
  4.1 14.0 %collective-permute-start = (f32[8,128,128]{2,1,0:T(8,128)}, f32[8,128,128]{2,1,0:T(8,128)}, u32[]{:S(2)}, u32[]{:S(2)}) collective-permute-start(f32[8,128,128]{2,1,0:T(8,128)} %fusion.17), channel_id=1, source_target_pairs={{0,4},{4,0},{8,12},{12,8},{16,20},{20,16},{24,28},{28,24},{1,5},{5... | collective-permute-start | bytes 1572872 | tf_op jit(solution)/shard_map/ppermute | solution.py:19
  19.2 12.9 %collective-permute-start.1 = (f32[8,128,128]{2,1,0:T(8,128)S(1)}, f32[8,128,128]{2,1,0:T(8,128)S(1)}, u32[]{:S(2)}, u32[]{:S(2)}) collective-permute-start(f32[8,128,128]{2,1,0:T(8,128)S(1)} %fusion.34), channel_id=1, source_target_pairs={{0,8},{8,0},{4,12},{12,4},{16,24},{24,16},{20,28},{28,20},{1,9},{9... | collective-permute-start | bytes 1572872 | tf_op jit(solution)/shard_map/ppermute | solution.py:19
  32.1 14.8 %copy-start.2 = (f32[2,8,256,128]{2,3,1,0:T(8,128)S(1)}, f32[2,8,256,128]{2,3,1,0:T(8,128)}, u32[]{:S(2)}) copy-start(f32[2,8,256,128]{2,3,1,0:T(8,128)} %fusion.5) | copy-start | bytes 6291460
  32.1 14.8 %collective-permute-start.2 = (bf16[8,128,128]{2,1,0:T(8,128)(2,1)S(1)}, bf16[8,128,128]{2,1,0:T(8,128)(2,1)S(1)}, u32[]{:S(2)}, u32[]{:S(2)}) collective-permute-start(bf16[8,128,128]{2,1,0:T(8,128)(2,1)S(1)} %add_convert_fusion), channel_id=1, source_target_pairs={{0,16},{4,20},{8,24},{12,28},{1,17},{5,21},{9,25},{13,29},{2,18},{... | collective-permute-start | bytes 786440 | tf_op jit(solution)/shard_map/ppermute | solution.py:25
  56.1 2.1 %copy-start.6 = (f32[1024]{0:T(1024)S(1)}, f32[1024]{0:T(1024)}, u32[]{:S(2)}) copy-start(f32[1024]{0:T(1024)} %param.9) | copy-start | bytes 12292
where the time goes:
time: 60 us; the launch traced here: 59.7 us
  waiting for transfers between devices  32.2 us (54%)
  matrix products  8.38 us (14%)
  blocking collectives  6.83 us (11%)
  local copies, waits for them, and re-layouts  5.2 us (9%)
  starting transfers between devices  3.46 us (6%)
  other arithmetic  3.45 us (6%)
    ppermute x2, waiting for transfers between devices, swapped(): return lax.ppermute(block, axis, route)  19.3 us
    ppermute x1, waiting for transfers between devices, shifted(): return lax.ppermute(block, axis, route)  12.8 us
    psum x1, blocking collectives, local(): total_squares = lax.psum(squares, 'head')  6.83 us
    dot_general x1, matrix products, local(): jnp.einsum('chts,cshv->cthv', attn_probs, value_blocks, preferred_element...  4.22 us
    dot_general x3, matrix products, local(): jnp.einsum('lwnx,nxq->lwnq', query_block_list, state_per_level, preferred...  3.39 us
    unnamed x18, local copies, waits for them, and re-layouts  2.36 us
    add x1, local copies, waits for them, and re-layouts, local(): combined + weights_here[1 + local_bits + number][..., None] * state_readout  2.12 us
    ppermute x2, starting transfers between devices, swapped(): return lax.ppermute(block, axis, route)  2.03 us
  transfers between devices with their start and end apart: 3, of which 3 were waited for; matrix products, arithmetic and copies ran while one was open for 10% of the time, Pallas kernels for 0%

commit v1 on v0

--- a/solution.py
+++ b/solution.py
@@ -91,7 +91,7 @@
         )
         combined = combined + weights_here[1 + local_bits + number][..., None] * state_readout
     squares = jnp.sum(combined * combined, axis=(2, 3)).reshape(tok_rows)
-    total_squares = lax.psum(squares, "head")
+    total_squares = jnp.sum(lax.all_gather(squares, "head"), axis=0)
     inverse_rms = lax.rsqrt(total_squares / D + EPSILON)
     flat_out = combined.reshape(tok_rows, heads_here * HEAD_DIM)
     mixed_out = flat_out * inverse_rms[:, None] * norm_gain[None, :]

time: 60 us -> 58.9 us (0.982)
  blocking collectives: 6.83 us -> 5.18 us
    psum x1 -> x0, blocking collectives: 6.83 us -> none  [local(): total_squares = lax.psum(squares, 'head')]
    all_gather x0 -> x1, blocking collectives: none -> 5.18 us  [local(): total_squares = jnp.sum(lax.all_gather(squares, 'head'), axis=0)]
where the time goes in v1:
time: 58.9 us; the launch traced here: 58.1 us
  waiting for transfers between devices  32.2 us (55%)
  matrix products  8.38 us (14%)
  local copies, waits for them, and re-layouts  5.21 us (9%)
  blocking collectives  5.18 us (9%)
  other arithmetic  3.47 us (6%)
  starting transfers between devices  3.46 us (6%)
    ppermute x2, waiting for transfers between devices, swapped(): return lax.ppermute(block, axis, route)  19.3 us
    ppermute x1, waiting for transfers between devices, shifted(): return lax.ppermute(block, axis, route)  12.8 us
    all_gather x1, blocking collectives, local(): total_squares = jnp.sum(lax.all_gather(squares, 'head'), axis=0)  5.18 us
    dot_general x1, matrix products, local(): jnp.einsum('chts,cshv->cthv', attn_probs, value_blocks, preferred_element...  4.22 us
    dot_general x3, matrix products, local(): jnp.einsum('lwnx,nxq->lwnq', query_block_list, state_per_level, preferred...  3.39 us
    unnamed x18, local copies, waits for them, and re-layouts  2.38 us
    add x1, local copies, waits for them, and re-layouts, local(): combined + weights_here[1 + local_bits + number][..., None] * state_readout  2.11 us
    ppermute x2, starting transfers between devices, swapped(): return lax.ppermute(block, axis, route)  2.03 us
  transfers between devices with their start and end apart: 3, of which 3 were waited for; matrix products, arithmetic and copies ran while one was open for 10% of the time, Pallas kernels for 0%

profile of v1, /device:TPU:24, one launch (start us, length us, event | category | flops | bytes accessed | tf_op | source)
XLA Modules:
  0.0 58.1 jit_solution(1504221375559089906)
XLA Ops:
  0.0 1.6 %copy.57 = bf16[64,8,8,128]{3,2,1,0:T(8,128)(2,1)S(1)} copy(bf16[64,8,8,128]{3,1,2,0:T(8,128)(2,1)} %bitcast.101) | data formatting | bytes 2097152
  1.6 0.7 %copy.37 = bf16[2,256,8,128]{1,3,2,0:T(8,128)(2,1)S(1)} copy(bf16[2,256,8,128]{3,2,1,0:T(8,128)(2,1)S(1)} %bitcast.100) | data formatting | bytes 2097152 | tf_op jit(solution)/shard_map/reshape | solution.py:34
  2.3 0.0 copy-start
  2.3 0.3 copy.58
  2.6 0.4 convolution_bitcast_fusion.1
  3.0 0.2 copy-done
  3.2 0.8 %fusion.17 = f32[8,128,128]{2,1,0:T(8,128)} fusion(f32[1,2,8,128,128]{4,3,2,1,0:T(8,128)S(1)} %convolution_bitcast_fusion.1), kind=kLoop, calls=%fused_computation.27 | loop fusion | flops 131072 | bytes 1572864 | tf_op jit(solution)/shard_map/add | solution.py:73
  4.1 1.5 %collective-permute-start = (f32[8,128,128]{2,1,0:T(8,128)}, f32[8,128,128]{2,1,0:T(8,128)}, u32[]{:S(2)}, u32[]{:S(2)}) collective-permute-start(f32[8,128,128]{2,1,0:T(8,128)} %fusion.17), channel_id=1, source_target_pairs={{0,4},{4,0},{8,12},{12,8},{16,20},{20,16},{24,28},{28,24},{1,5},{5... | collective-permute-start | bytes 1572872 | tf_op jit(solution)/shard_map/ppermute | solution.py:19
  5.7 0.3 copy.56
  6.0 0.3 fusion.7
  6.4 4.2 %fusion.5 = f32[2,8,256,128]{2,3,1,0:T(8,128)} fusion(bf16[2,256,8,128]{1,3,2,0:T(8,128)(2,1)} %copy-done, pred[256,256]{1,0:T(8,128)(4,1)S(1)} %iota_compare_fusion, bf16[2,256,8,128]{3,2,1,0:T(8,128)(2,1)} %bitcast.99, bf16[2,256,8,128]{3,2,1,0:T(8,128)(2,1)S(1)} %bitcast.93), kind=kOutput, calls=%fused_computation.13 | convolution fusion | flops 538968064 | bytes 5308416 | tf_op jit(solution)/shard_map/chts,cshv->cthv/dot_general | solution.py:50
  10.6 7.5 %collective-permute-done = f32[8,128,128]{2,1,0:T(8,128)} collective-permute-done((f32[8,128,128]{2,1,0:T(8,128)}, f32[8,128,128]{2,1,0:T(8,128)}, u32[]{:S(2)}, u32[]{:S(2)}) %collective-permute-start) | collective-permute-done | bytes 524320 | tf_op jit(solution)/shard_map/ppermute | solution.py:19
  18.1 1.1 %fusion.34 = f32[8,128,128]{2,1,0:T(8,128)S(1)} fusion(f32[8,128,128]{2,1,0:T(8,128)} %collective-permute-done, f32[1,2,8,128,128]{4,3,2,1,0:T(8,128)S(1)} %convolution_bitcast_fusion.1), kind=kLoop, calls=%fused_computation.51 | loop fusion | flops 262144 | bytes 2097152 | tf_op jit(solution)/shard_map/add | solution.py:85
  19.2 0.5 collective-permute-start.1
  19.7 0.5 fusion.13
  20.2 11.8 %collective-permute-done.1 = f32[8,128,128]{2,1,0:T(8,128)S(1)} collective-permute-done((f32[8,128,128]{2,1,0:T(8,128)S(1)}, f32[8,128,128]{2,1,0:T(8,128)S(1)}, u32[]{:S(2)}, u32[]{:S(2)}) %collective-permute-start.1) | collective-permute-done | bytes 524320 | tf_op jit(solution)/shard_map/ppermute | solution.py:19
  32.1 0.1 add_convert_fusion
  32.1 1.4 %collective-permute-start.2 = (bf16[8,128,128]{2,1,0:T(8,128)(2,1)S(1)}, bf16[8,128,128]{2,1,0:T(8,128)(2,1)S(1)}, u32[]{:S(2)}, u32[]{:S(2)}) collective-permute-start(bf16[8,128,128]{2,1,0:T(8,128)(2,1)S(1)} %add_convert_fusion), channel_id=1, source_target_pairs={{0,16},{4,20},{8,24},{12,28},{1,17},{5,21},{9,25},{13,29},{2,18},{... | collective-permute-start | bytes 786440 | tf_op jit(solution)/shard_map/ppermute | solution.py:25
  33.6 0.5 fusion.11
  34.1 12.8 %collective-permute-done.2 = bf16[8,128,128]{2,1,0:T(8,128)(2,1)S(1)} collective-permute-done((bf16[8,128,128]{2,1,0:T(8,128)(2,1)S(1)}, bf16[8,128,128]{2,1,0:T(8,128)(2,1)S(1)}, u32[]{:S(2)}, u32[]{:S(2)}) %collective-permute-start.2) | collective-permute-done | bytes 262176 | tf_op jit(solution)/shard_map/ppermute | solution.py:25
  46.9 2.4 %multiply_reduce_fusion = (f32[2,256]{1,0:T(2,128)S(1)}, f32[2,256,8,128]{1,3,2,0:T(8,128)}) fusion(bf16[2,256,8,128]{3,2,1,0:T(8,128)(2,1)S(1)} %bitcast.96, bf16[8,128,128]{2,1,0:T(8,128)(2,1)S(1)} %collective-permute-done.2, f32[2,256,8]{1,2,0:T(8,128)S(1)} %get-tuple-element.6, f32[8,128,2,256]{3,1,0,2:T(8,128)S(1)} %fusion.11, ...), kind=kOutput, calls=%fused_computation.12 | convolution fusion | flops 139460096 | bytes 10815488 | tf_op jit(solution)/shard_map/lwnx,nxq->lwnq/dot_general | solution.py:89
  49.3 5.2 %all-gather = f32[4,1,512]{2,1,0:T(1,128)S(1)} all-gather(f32[1,1,512]{2,1,0:T(1,128)S(1)} %reshape.68), channel_id=1, replica_groups=mesh['seq'=8,'head'=4] {'head'}, dimensions={0}, use_global_device_ids=true | all-gather | bytes 10240 | tf_op jit(solution)/shard_map/all_gather | solution.py:94
  54.5 2.1 %copy.47 = f32[2,256,8,128]{3,2,1,0:T(8,128)S(1)} copy(f32[2,256,8,128]{1,3,2,0:T(8,128)} %get-tuple-element.10) | data formatting | bytes 4194304 | tf_op jit(solution)/shard_map/add | solution.py:92
  56.7 1.4 %fusion.1 = bf16[512,1024]{1,0:T(8,128)(2,1)} fusion(f32[64,8,8,128]{3,2,1,0:T(8,128)S(1)} %bitcast.97, f32[1024]{0:T(1024)S(1)} %copy-done.6, f32[512]{0:T(512)S(1)} %add_rsqrt_fusion), kind=kLoop, calls=%fused_computation.3 | loop fusion | flops 1572864 | bytes 3151872 | tf_op jit(solution)/shard_map/convert_element_type | solution.py:98
  (19 shorter events, 0.2 us)
Async XLA Ops:
  0.0 2.3 %copy-start.3 = (bf16[512,1024]{1,0:T(8,128)(2,1)S(1)}, bf16[512,1024]{1,0:T(8,128)(2,1)}, u32[]{:S(2)}) copy-start(bf16[512,1024]{1,0:T(8,128)(2,1)} %param.7) | copy-start | bytes 3145732
  2.3 1.0 %copy-start = (bf16[2,256,8,128]{1,3,2,0:T(8,128)(2,1)}, bf16[2,256,8,128]{1,3,2,0:T(8,128)(2,1)S(1)}, u32[]{:S(2)}) copy-start(bf16[2,256,8,128]{1,3,2,0:T(8,128)(2,1)S(1)} %copy.37) | copy-start | bytes 3145732
  2.6 1.5 %copy-start.1 = (bf16[64,8,8,128]{3,2,1,0:T(8,128)(2,1)}, bf16[64,8,8,128]{3,2,1,0:T(8,128)(2,1)S(1)}, u32[]{:S(2)}) copy-start(bf16[64,8,8,128]{3,2,1,0:T(8,128)(2,1)S(1)} %copy.58) | copy-start | bytes 3145732
  2.6 3.1 %copy-start.5 = (f32[5,8,512]{2,1,0:T(8,128)S(1)}, f32[5,8,512]{2,1,0:T(8,128)}, u32[]{:S(2)}) copy-start(f32[5,8,512]{2,1,0:T(8,128)} %param.8) | copy-start | bytes 245764
  2.6 3.1 %copy-start.4 = (bf16[512,1024]{1,0:T(8,128)(2,1)S(1)}, bf16[512,1024]{1,0:T(8,128)(2,1)}, u32[]{:S(2)}) copy-start(bf16[512,1024]{1,0:T(8,128)(2,1)} %param.5) | copy-start | bytes 3145732
  4.1 14.0 %collective-permute-start = (f32[8,128,128]{2,1,0:T(8,128)}, f32[8,128,128]{2,1,0:T(8,128)}, u32[]{:S(2)}, u32[]{:S(2)}) collective-permute-start(f32[8,128,128]{2,1,0:T(8,128)} %fusion.17), channel_id=1, source_target_pairs={{0,4},{4,0},{8,12},{12,8},{16,20},{20,16},{24,28},{28,24},{1,5},{5... | collective-permute-start | bytes 1572872 | tf_op jit(solution)/shard_map/ppermute | solution.py:19
  19.2 12.9 %collective-permute-start.1 = (f32[8,128,128]{2,1,0:T(8,128)S(1)}, f32[8,128,128]{2,1,0:T(8,128)S(1)}, u32[]{:S(2)}, u32[]{:S(2)}) collective-permute-start(f32[8,128,128]{2,1,0:T(8,128)S(1)} %fusion.34), channel_id=1, source_target_pairs={{0,8},{8,0},{4,12},{12,4},{16,24},{24,16},{20,28},{28,20},{1,9},{9... | collective-permute-start | bytes 1572872 | tf_op jit(solution)/shard_map/ppermute | solution.py:19
  32.1 14.8 %copy-start.2 = (f32[2,8,256,128]{2,3,1,0:T(8,128)S(1)}, f32[2,8,256,128]{2,3,1,0:T(8,128)}, u32[]{:S(2)}) copy-start(f32[2,8,256,128]{2,3,1,0:T(8,128)} %fusion.5) | copy-start | bytes 6291460
  32.1 14.8 %collective-permute-start.2 = (bf16[8,128,128]{2,1,0:T(8,128)(2,1)S(1)}, bf16[8,128,128]{2,1,0:T(8,128)(2,1)S(1)}, u32[]{:S(2)}, u32[]{:S(2)}) collective-permute-start(bf16[8,128,128]{2,1,0:T(8,128)(2,1)S(1)} %add_convert_fusion), channel_id=1, source_target_pairs={{0,16},{4,20},{8,24},{12,28},{1,17},{5,21},{9,25},{13,29},{2,18},{... | collective-permute-start | bytes 786440 | tf_op jit(solution)/shard_map/ppermute | solution.py:25
  54.5 2.1 %copy-start.6 = (f32[1024]{0:T(1024)S(1)}, f32[1024]{0:T(1024)}, u32[]{:S(2)}) copy-start(f32[1024]{0:T(1024)} %param.9) | copy-start | bytes 12292
